TPU v7x, 32 devices: a whole 2x2x4 slice. The times are simulated.
32 devices in a mesh: ctx: 4 (over x, core), exp: 4 (over z), tp: 2 (over y).
Axes of the slice: x: 2, y: 2, z: 4, core: 2. Of those that a mesh axis runs over, the one named last changes fastest.
Arguments:
- mamba_in: bfloat16 [512, 8192], P('ctx', ('exp', 'tp')), may hold values from -6 to 6
- gate_in: bfloat16 [512, 8192], P('ctx', ('exp', 'tp')), may hold values from -6 to 6
- step_size: float32 [512, 8192], P('ctx', ('exp', 'tp')), may hold values from 0 to 2
- input_proj: float32 [16, 512], P(None, 'ctx'), may hold values from -6 to 6
- output_proj: float32 [16, 512], P(None, 'ctx'), may hold values from -6 to 6
- decay_log: float32 [16, 8192], P(None, ('exp', 'tp')), may hold values from -0.7 to 0.7
- skip_gain: float32 [8192], P(('exp', 'tp')), may hold values from 0.5 to 2
- out_weight: bfloat16 [8192, 2048], P(('exp', 'tp')), may hold values from -0.0625 to 0.0625
- residual: bfloat16 [512, 2048], P('ctx', ('exp', 'tp')), may hold values from -6 to 6
- routes: int32 [512, 2], P('ctx'), may hold values from 0 to 3, all different within a row; in each aligned block of 128 rows (0 to 127, 128 to 255, ...) at most 128 rows name the same one
- norm_gain: float32 [2048], replicated, may hold values from 0.25 to 1.75
- w_gate: bfloat16 [4, 2048, 14336], P('exp', None, ('ctx', 'tp')), may hold values from -0.125 to 0.125
- w_up: bfloat16 [4, 2048, 14336], P('exp', None, ('ctx', 'tp')), may hold values from -0.125 to 0.125
- w_down: bfloat16 [4, 14336, 2048], P('exp', 'ctx', 'tp'), may hold values from -0.046875 to 0.046875
Outputs:
- expert_out: bfloat16 [4, 4, 128, 2048], P('ctx', 'exp', None, 'tp')
Inputs may be any that keep to these rules, and one draw needn't show every extreme that they name: `routes`: within each aligned block of 128 positions no expert is named by more than 128 of the block's rows, a bound that some expert reaches in some block.
All inputs are finite; a program needn't handle non-finite values.
Results may differ from a plain program's by a relative error of at most 0.015.
Values may be sent and summed in bfloat16 or wider, within the bound.
A program may use at most 128 MiB of HBM per device.

v0:
```python
import jax
import jax.numpy as jnp
from jax import lax
from jax.sharding import PartitionSpec as P


def prefix_2(value, axis, join, neutral):
    count, mine = (lax.axis_size(axis), lax.axis_index(axis))
    pieces = jax.tree.map(lambda part: lax.all_gather(part, axis), value)
    so_far = jax.tree.map(
        lambda part, zero: jnp.full_like(part, 0) + jnp.asarray(zero, part.dtype), value, neutral
    )

    def step(position, so_far):
        longer = join(so_far, jax.tree.map(lambda part: part[position], pieces))
        return jax.tree.map(lambda new, old: jnp.where(position < mine, new, old), longer, so_far)

    return lax.fori_loop(0, count - 1, step, so_far)


def route_rows(routes, capacity, experts):
    flattened = routes.reshape(-1)
    one_hot = (flattened[:, None] == jnp.arange(experts, dtype=jnp.int32)[None, :]).astype(
        jnp.int32
    )
    earlier = jnp.cumsum(one_hot, axis=0) - one_hot
    slot_index = jnp.sum(earlier * one_hot, axis=1)
    return (flattened * capacity + slot_index).reshape(routes.shape)


def pick_rows(row_ids, first_row, row_count):
    targets = first_row + jnp.arange(row_count, dtype=jnp.int32)
    matches = row_ids[None, :, :] == targets[:, None, None]
    return jnp.sum(matches.astype(jnp.float32), axis=2).astype(jnp.bfloat16)


def rms_scale(row_data, norm_gain):
    mean_sq = jnp.mean(row_data * row_data, axis=1, keepdims=True)
    return (row_data * lax.rsqrt(mean_sq + 1e-06) * norm_gain).astype(jnp.bfloat16)


def combine_link(earlier, later_link):
    return (earlier[0] * later_link[0], later_link[0] * earlier[1] + later_link[1])


def body(
    mamba_in,
    gate_in,
    step_size,
    input_proj,
    output_proj,
    decay_log,
    skip_gain,
    out_weight,
    residual,
    routes,
    norm_gain,
    w_gate,
    w_up,
    w_down,
):
    length = mamba_in.shape[0]
    decay_rate = -jnp.exp(decay_log)
    signal = mamba_in.astype(jnp.float32)
    decays = jnp.exp(step_size[:, None, :] * decay_rate[None, :, :])
    driving = (step_size * signal)[:, None, :] * jnp.transpose(input_proj)[:, :, None]
    cum_decay, local_state = lax.associative_scan(combine_link, (decays, driving), axis=0)
    summary = (cum_decay[-1], local_state[-1])
    identity = (jnp.ones_like(summary[0]), jnp.zeros_like(summary[1]))
    prefix = prefix_2(summary, "ctx", combine_link, identity)
    incoming = prefix[1]
    full_state = local_state + cum_decay * incoming[None, :, :]
    readout = jnp.sum(jnp.transpose(output_proj)[:, :, None] * full_state, axis=1)
    gated_out = ((readout + skip_gain * signal) * jax.nn.silu(gate_in.astype(jnp.float32))).astype(
        jnp.bfloat16
    )
    experts = lax.axis_size("exp")
    top_count = routes.shape[1]
    capacity = length * top_count * 2 // experts
    row_ids = route_rows(routes, capacity, experts)
    rows_here = capacity // lax.axis_size("tp")
    col_width = residual.shape[1]
    model_width = out_weight.shape[1]
    offset = lax.axis_index(("exp", "tp")) * col_width
    mixed_rows = jnp.dot(gated_out, out_weight, preferred_element_type=jnp.float32)
    lifted = residual.astype(jnp.float32)
    placed = jnp.zeros((lifted.shape[0], model_width), jnp.float32)
    token_part = lax.psum_scatter(
        mixed_rows + lax.dynamic_update_slice_in_dim(placed, lifted, offset, 1),
        ("exp", "tp"),
        scatter_dimension=0,
        tiled=True,
    )
    every_token = lax.all_gather(
        rms_scale(token_part, norm_gain), ("exp", "tp"), axis=0, tiled=True
    )
    picker = pick_rows(row_ids, lax.axis_index(("exp", "tp")) * rows_here, rows_here)
    normed = jnp.dot(picker, every_token, preferred_element_type=jnp.float32).astype(jnp.bfloat16)
    row_block = lax.all_gather(normed, ("ctx", "tp"), axis=0, tiled=True)
    gate_part = jnp.dot(row_block, w_gate[0], preferred_element_type=jnp.float32)
    up_part = jnp.dot(row_block, w_up[0], preferred_element_type=jnp.float32)
    hidden = (jax.nn.silu(gate_part) * up_part).astype(jnp.bfloat16)
    local_down = w_down[0]
    partial_out = jnp.dot(
        lax.all_gather(hidden, "tp", axis=1, tiled=True),
        local_down,
        preferred_element_type=jnp.float32,
    )
    result = lax.psum_scatter(
        partial_out.astype(jnp.bfloat16), "ctx", scatter_dimension=0, tiled=True
    )
    return result[None, None]


def solution(mesh):
    in_specs = (
        P("ctx", ("exp", "tp")),
        P("ctx", ("exp", "tp")),
        P("ctx", ("exp", "tp")),
        P(None, "ctx"),
        P(None, "ctx"),
        P(None, ("exp", "tp")),
        P(("exp", "tp")),
        P(("exp", "tp"), None),
        P("ctx", ("exp", "tp")),
        P("ctx", None),
        P(),
        P("exp", None, ("ctx", "tp")),
        P("exp", None, ("ctx", "tp")),
        P("exp", "ctx", "tp"),
    )
    out_specs = P("ctx", "exp", None, "tp")
    return jax.shard_map(body, mesh=mesh, in_specs=in_specs, out_specs=out_specs, check_vma=False)
```

profile of v0, /device:TPU:0, one launch (start us, length us, event | category | flops | bytes accessed | tf_op | source)
XLA Modules:
  0.0 632.6 jit_solution(5301947905542843540)
XLA Ops:
  9.4 7.6 %multiply_exponential_fusion = (f32[128,16,1024]{2,1,0:T(8,128)}, f32[128,16,1024]{2,1,0:T(8,128)}) fusion(f32[16,1024]{1,0:T(8,128)S(1)} %exponential_negate_fusion, f32[128,1024]{1,0:T(8,128)} %param.18, f32[128,16]{1,0:T(8,128)S(1)} %copy.51, f32[128,1024]{1,0:T(8,128)S(1)} %convert_multiply_fusion.2), kind=kLoop, calls=%fused_computation.4 | loop fusion | flops 4194304 | bytes 17899520 | tf_op jit(solution)/shard_map/exp | solution.py:65
  17.0 10.4 %slice_add_fusion = (f32[64,16,1024]{2,1,0:T(8,128)}, f32[64,16,1024]{2,1,0:T(8,128)S(1)}) fusion(f32[128,16,1024]{2,1,0:T(8,128)} %get-tuple-element.159, f32[128,16,1024]{2,1,0:T(8,128)} %get-tuple-element.158), kind=kLoop, calls=%fused_computation.14 | loop fusion | flops 3145728 | bytes 25165824 | tf_op jit(solution)/shard_map/add | solution.py:43
  27.3 4.7 slice_add_fusion.1
  44.0 3.7 pad.91
  47.7 2.1 pad.105
  49.8 2.1 pad.104
  51.9 2.0 add.233
  54.0 2.6 fusion.21
  57.5 5.7 pad.93
  63.2 1.9 pad_maximum_fusion.6
  65.0 5.7 pad.92
  70.7 3.5 pad.107
  74.3 3.5 pad.106
  77.8 2.7 add.235
  80.5 4.1 fusion.14
  88.7 7.0 %pad.94 = f32[32,16,1024]{2,1,0:T(8,128)S(1)} pad(f32[16,16,1024]{2,1,0:T(8,128)} %pad_maximum_fusion.4, f32[]{:T(128)} %constant.57.clone.1), padding=0_1_1x0_0_0x0_0_0 | pad | bytes 3145732 | tf_op jit(solution)/shard_map/pad | solution.py:67
  95.6 6.3 pad.95
  101.9 10.2 %pad.109 = f32[32,16,1024]{2,1,0:T(8,128)} pad(f32[16,16,1024]{2,1,0:T(8,128)} %add.245, f32[]{:T(128)} %constant.57.clone.1), padding=1_0_1x0_0_0x0_0_0 | pad | bytes 3145732 | tf_op jit(solution)/shard_map/pad | solution.py:67
  113.4 6.3 pad.108
  119.7 3.5 add.237
  124.0 6.3 fusion.10
  130.3 1.8 add.246
  133.8 12.0 %pad.97 = f32[64,16,1024]{2,1,0:T(8,128)} pad(f32[32,16,1024]{2,1,0:T(8,128)S(1)} %copy-done.11, f32[]{:T(128)} %constant.57.clone.1), padding=1_0_1x0_0_0x0_0_0 | pad | bytes 6291460 | tf_op jit(solution)/shard_map/pad | solution.py:67
  145.8 3.2 pad_maximum_fusion.2
  149.0 18.6 %pad.96 = f32[64,16,1024]{2,1,0:T(8,128)} pad(f32[32,16,1024]{2,1,0:T(8,128)} %pad_maximum_fusion.2, f32[]{:T(128)} %constant.57.clone.1), padding=0_1_1x0_0_0x0_0_0 | pad | bytes 6291460 | tf_op jit(solution)/shard_map/pad | solution.py:67
  167.6 12.1 %pad.111 = f32[64,16,1024]{2,1,0:T(8,128)} pad(f32[32,16,1024]{2,1,0:T(8,128)S(1)} %copy-done.12, f32[]{:T(128)} %constant.57.clone.1), padding=1_0_1x0_0_0x0_0_0 | pad | bytes 6291460 | tf_op jit(solution)/shard_map/pad | solution.py:67
  181.3 12.0 %pad.110 = f32[64,16,1024]{2,1,0:T(8,128)} pad(f32[32,16,1024]{2,1,0:T(8,128)S(1)} %pad_maximum_fusion.3, f32[]{:T(128)} %constant.57.clone.1), padding=0_1_1x0_0_0x0_0_0 | pad | bytes 6291460 | tf_op jit(solution)/shard_map/pad | solution.py:67
  193.3 7.1 %add.247 = f32[64,16,1024]{2,1,0:T(8,128)} add(f32[64,16,1024]{2,1,0:T(8,128)} %pad.110, f32[64,16,1024]{2,1,0:T(8,128)} %pad.111) | non-fusion elementwise | flops 1048576 | bytes 12582912 | tf_op jit(solution)/shard_map/add | solution.py:67
  201.9 8.1 %fusion.7 = (f32[63,16,1024]{2,1,0:T(8,128)}, f32[63,16,1024]{2,1,0:T(8,128)}) fusion(f32[64,16,1024]{2,1,0:T(8,128)S(1)} %copy-done, f32[64,16,1024]{2,1,0:T(8,128)S(1)} %copy-done.1, f32[128,16,1024]{2,1,0:T(8,128)} %get-tuple-element.159, f32[128,16,1024]{2,1,0:T(8,128)} %get-tuple-element.158, f32[64,16,1024]{2,1,0:T(8,128)S(1)} %copy-done.2, ...), kind=kLoop, calls=%fused_computation.18 | loop fusion | flops 5160960 | bytes 33030144 | tf_op jit(solution)/shard_map/add | solution.py:43
  210.0 3.1 add.239
  213.1 4.7 pad_maximum_fusion.1
  217.8 35.5 %pad.112 = f32[128,16,1024]{2,1,0:T(8,128)} pad(f32[64,16,1024]{2,1,0:T(8,128)} %pad_maximum_fusion.1, f32[]{:T(128)} %constant.57.clone.1), padding=0_1_1x0_0_0x0_0_0 | pad | bytes 12582916 | tf_op jit(solution)/shard_map/pad | solution.py:67
  253.3 35.5 %pad.113 = f32[128,16,1024]{2,1,0:T(8,128)} pad(f32[64,16,1024]{2,1,0:T(8,128)} %add.247, f32[]{:T(128)} %constant.57.clone.1), padding=1_0_1x0_0_0x0_0_0 | pad | bytes 12582916 | tf_op jit(solution)/shard_map/pad | solution.py:67
  288.8 4.7 pad_maximum_fusion
  293.5 35.5 %pad.98 = f32[128,16,1024]{2,1,0:T(8,128)} pad(f32[64,16,1024]{2,1,0:T(8,128)} %pad_maximum_fusion, f32[]{:T(128)} %constant.57.clone.1), padding=0_1_1x0_0_0x0_0_0 | pad | bytes 12582916 | tf_op jit(solution)/shard_map/pad | solution.py:67
  329.0 35.5 %pad.99 = f32[128,16,1024]{2,1,0:T(8,128)} pad(f32[64,16,1024]{2,1,0:T(8,128)} %add.239, f32[]{:T(128)} %constant.57.clone.1), padding=1_0_1x0_0_0x0_0_0 | pad | bytes 12582916 | tf_op jit(solution)/shard_map/pad | solution.py:67
  365.4 7.2 %all_gather.15 = f32[4,16,1024]{2,1,0:T(8,128)S(1)} all-gather(f32[1,16,1024]{2,1,0:T(8,128)S(1)} %slice_add_fusion.7), channel_id=1, replica_groups=mesh['ctx'=4,'exp'=4,'tp'=2] {'ctx'}, dimensions={0}, use_global_device_ids=true | all-gather | bytes 327680 | tf_op jit(solution)/shard_map/all_gather | solution.py:9
  373.5 5.9 all_gather.16
  379.6 13.9 %multiply_reduce_fusion = f32[128,1024]{1,0:T(8,128)S(1)} fusion(f32[128,16,1024]{2,1,0:T(8,128)} %pad.112, f32[128,16,1024]{2,1,0:T(8,128)} %pad.113, f32[128,16,1024]{2,1,0:T(8,128)} %pad.98, f32[128,16,1024]{2,1,0:T(8,128)} %pad.99, f32[16,1024]{1,0:T(8,128)S(1)} %get-tuple-element.99, f32[128,16]{1,0:T(8,128)S(1)} %copy.50), kind=kLoop, calls=%fused_computation.3 | loop fusion | flops 12451840 | bytes 34152448 | tf_op jit(solution)/shard_map/reduce_sum | solution.py:73
  393.6 3.0 fusion.22
  400.1 63.2 %reduce-scatter.3.cloned.1.call-done = f32[16,2048]{1,0:T(8,128)} async-done(((f32[128,2048]{1,0:T(8,128)}), f32[16,2048]{1,0:T(8,128)}) %reduce-scatter.3.cloned.1.call-update) | async-done | bytes 131088 | tf_op jit(solution)/shard_map/reduce_scatter | solution.py:88
  465.4 31.5 %all_gather.17 = bf16[128,2048]{1,0:T(8,128)(2,1)S(1)} all-gather(bf16[16,2048]{1,0:T(8,128)(2,1)S(1)} %multiply_convert_fusion.1), channel_id=1, replica_groups=mesh['ctx'=4,'exp'=4,'tp'=2] {'exp','tp'}, dimensions={0}, use_global_device_ids=true | all-gather | bytes 589824 | tf_op jit(solution)/shard_map/all_gather | solution.py:94
  498.2 26.5 %all-gather.3.cloned.1.call-done = bf16[512,2048]{1,0:T(8,128)(2,1)} async-done(((bf16[64,2048]{1,0:T(8,128)(2,1)}), bf16[512,2048]{1,0:T(8,128)(2,1)}) %all-gather.3.cloned.1.call-update) | async-done | bytes 2097168 | tf_op jit(solution)/shard_map/all_gather | solution.py:99
  524.7 7.8 %fusion.5 = f32[512,1792]{1,0:T(8,128)S(1)} fusion(bf16[512,2048]{1,0:T(8,128)(2,1)} %all-gather.3.cloned.1.call-done, bf16[1,2048,1792]{2,1,0:T(8,128)(2,1)} %param.27), kind=kOutput, calls=%fused_computation.9 | convolution fusion | flops 3758096384 | bytes 13107200 | tf_op jit(solution)/shard_map/dot_general | solution.py:100
  532.5 8.5 %multiply_convert_fusion = bf16[512,1792]{1,0:T(8,128)(2,1)} fusion(f32[512,1792]{1,0:T(8,128)S(1)} %fusion.5, bf16[512,2048]{1,0:T(8,128)(2,1)S(1)} %copy-done.25, bf16[1,2048,1792]{2,1,0:T(8,128)(2,1)} %param.28), kind=kOutput, calls=%fused_computation.19 | convolution fusion | flops 3763601408 | bytes 14942208 | tf_op jit(solution)/shard_map/dot_general | solution.py:101
  541.1 50.9 %all-gather.5.cloned.1.call-done = bf16[512,3584]{1,0:T(8,128)(2,1)} async-done(((bf16[512,1792]{1,0:T(8,128)(2,1)}), bf16[512,3584]{1,0:T(8,128)(2,1)}) %all-gather.5.cloned.1.call-update) | async-done | bytes 3670032 | tf_op jit(solution)/shard_map/all_gather | solution.py:105
  592.0 9.1 %fusion.11 = bf16[512,1024]{1,0:T(8,128)(2,1)} fusion(bf16[512,3584]{1,0:T(8,128)(2,1)} %all-gather.5.cloned.1.call-done, bf16[1,3584,1024]{2,1,0:T(8,128)(2,1)} %param.29), kind=kOutput, calls=%fused_computation.28 | convolution fusion | flops 3758620672 | bytes 12058624 | tf_op jit(solution)/shard_map/dot_general | solution.py:104
  601.1 25.0 %reduce-scatter.5.cloned.1.call-done = bf16[128,1024]{1,0:T(8,128)(2,1)} async-done(((bf16[512,1024]{1,0:T(8,128)(2,1)}), bf16[128,1024]{1,0:T(8,128)(2,1)}) %reduce-scatter.5.cloned.1.call-update) | async-done | bytes 262160 | tf_op jit(solution)/shard_map/reduce_scatter | solution.py:109
  (133 shorter events, 35.3 us)
Async XLA Ops:
  6.5 456.8 %reduce-scatter.3.cloned.1.call-start = ((), (), s32[]{:S(2)}) async-start(), calls=%async_computation.2 | async-start | bytes 1179648 | tf_op jit(solution)/shard_map/reduce_scatter | solution.py:88
  27.3 4.7 copy-start.3
  32.0 1.4 copy-start.8
  32.5 1.2 copy-start.13
  32.5 1.6 copy-start.14
  33.4 1.5 copy-start.18
  51.9 4.6 copy-start.15
  51.9 4.6 copy-start.16
  80.5 4.1 copy-start.9
  80.5 4.1 copy-start.10
  84.7 10.9 %copy-start.17 = (f32[16,16,1024]{2,1,0:T(8,128)S(1)}, f32[16,16,1024]{2,1,0:T(8,128)}, u32[]{:S(2)}) copy-start(f32[16,16,1024]{2,1,0:T(8,128)} %add.235) | copy-start | bytes 3145732
  119.7 3.5 copy-start.4
  119.7 4.3 copy-start.5
  124.0 6.3 %copy-start.6 = (f32[32,16,1024]{2,1,0:T(8,128)S(1)}, f32[32,16,1024]{2,1,0:T(8,128)}, u32[]{:S(2)}) copy-start(f32[32,16,1024]{2,1,0:T(8,128)} %pad.109) | copy-start | bytes 6291460
  124.0 6.3 %copy-start.7 = (f32[32,16,1024]{2,1,0:T(8,128)S(1)}, f32[32,16,1024]{2,1,0:T(8,128)}, u32[]{:S(2)}) copy-start(f32[32,16,1024]{2,1,0:T(8,128)} %pad.108) | copy-start | bytes 6291460
  130.3 3.5 copy-start.11
  149.0 18.6 %copy-start.12 = (f32[32,16,1024]{2,1,0:T(8,128)S(1)}, f32[32,16,1024]{2,1,0:T(8,128)}, u32[]{:S(2)}) copy-start(f32[32,16,1024]{2,1,0:T(8,128)} %add.246) | copy-start | bytes 6291460
  193.3 7.1 %copy-start = (f32[64,16,1024]{2,1,0:T(8,128)S(1)}, f32[64,16,1024]{2,1,0:T(8,128)}, u32[]{:S(2)}) copy-start(f32[64,16,1024]{2,1,0:T(8,128)} %pad.97) | copy-start | bytes 12582916
  193.3 7.1 %copy-start.1 = (f32[64,16,1024]{2,1,0:T(8,128)S(1)}, f32[64,16,1024]{2,1,0:T(8,128)}, u32[]{:S(2)}) copy-start(f32[64,16,1024]{2,1,0:T(8,128)} %pad.96) | copy-start | bytes 12582916
  193.3 8.6 %copy-start.2 = (f32[64,16,1024]{2,1,0:T(8,128)S(1)}, f32[64,16,1024]{2,1,0:T(8,128)}, u32[]{:S(2)}) copy-start(f32[64,16,1024]{2,1,0:T(8,128)} %pad.111) | copy-start | bytes 12582916
  329.0 50.4 %copy-start.22 = (f32[16,128]{1,0:T(8,128)S(1)}, f32[16,128]{1,0:T(8,128)}, u32[]{:S(2)}) copy-start(f32[16,128]{1,0:T(8,128)} %param.20) | copy-start | bytes 24580
  379.6 14.0 %copy-start.20 = (bf16[128,1024]{1,0:T(8,128)(2,1)S(1)}, bf16[128,1024]{1,0:T(8,128)(2,1)}, u32[]{:S(2)}) copy-start(bf16[128,1024]{1,0:T(8,128)(2,1)} %param.16) | copy-start | bytes 786436
  379.6 14.0 %copy-start.26 = (bf16[128,1024]{1,0:T(8,128)(2,1)S(1)}, bf16[128,1024]{1,0:T(8,128)(2,1)}, u32[]{:S(2)}) copy-start(bf16[128,1024]{1,0:T(8,128)(2,1)} %param.17) | copy-start | bytes 786436
  379.6 14.0 %copy-start.27 = (f32[1024]{0:T(1024)S(1)}, f32[1024]{0:T(1024)}, u32[]{:S(2)}) copy-start(f32[1024]{0:T(1024)} %param.22) | copy-start | bytes 12292
  393.5 3.1 copy-start.21
  393.5 4.2 copy-start.24
  393.6 70.8 %copy-start.23 = (f32[2048]{0:T(1024)S(1)}, f32[2048]{0:T(1024)}, u32[]{:S(2)}) copy-start(f32[2048]{0:T(1024)} %param.26) | copy-start | bytes 24580
  396.7 1.0 copy-start.19
  397.7 127.0 %all-gather.3.cloned.1.call-start = ((), (), s32[]{:S(2)}) async-start(), calls=%async_computation.3 | async-start | bytes 2359296 | tf_op jit(solution)/shard_map/all_gather | solution.py:99
  497.9 94.1 %all-gather.5.cloned.1.call-start = ((), (), s32[]{:S(2)}) async-start(), calls=%async_computation.4 | async-start | bytes 5505024 | tf_op jit(solution)/shard_map/all_gather | solution.py:105
  524.7 7.8 %copy-start.25 = (bf16[512,2048]{1,0:T(8,128)(2,1)S(1)}, bf16[512,2048]{1,0:T(8,128)(2,1)}, u32[]{:S(2)}) copy-start(bf16[512,2048]{1,0:T(8,128)(2,1)} %all-gather.3.cloned.1.call-done) | copy-start | bytes 6291460
  541.0 85.1 %reduce-scatter.5.cloned.1.call-start = ((), (), s32[]{:S(2)}) async-start(), calls=%async_computation.5 | async-start | bytes 1310720 | tf_op jit(solution)/shard_map/reduce_scatter | solution.py:109
Sparse Core Ops, SparseCore 0:
  397.8 65.5 reduce-scatter.2
  498.0 26.6 all-gather.2
  541.1 50.8 all-gather.4
  601.3 24.8 reduce-scatter.4
where the time goes:
time: 646 us; the launch traced here: 633 us
  local copies, waits for them, and re-layouts  268 us (41%)
  waiting for transfers between devices  166 us (26%)
  other arithmetic  111 us (17%)
  blocking collectives  44.6 us (7%)
  matrix products  29.3 us (5%)
  between operations  13.6 us (2%)
    pad x24, local copies, waits for them, and re-layouts, body(): lax.associative_scan(combine_link, (decays, driving), axis=0)  255 us
    reduce_scatter x1, waiting for transfers between devices, body(): lax.psum_scatter(mixed_rows + lax.dynamic_update_slice_in_dim(placed, lif...  63.2 us
    all_gather x1, waiting for transfers between devices, body(): lax.all_gather(hidden, 'tp', axis=1, tiled=True)  50.9 us
    add x12, other arithmetic, combine_link(): later_link[0] * earlier[1] + later_link[1]  38.1 us
    all_gather x1, blocking collectives, body(): lax.all_gather(rms_scale(token_part, norm_gain), ('exp', 'tp'), axis=0, t...  31.5 us
    all_gather x1, waiting for transfers between devices, body(): row_block = lax.all_gather(normed, ('ctx', 'tp'), axis=0, tiled=True)  26.5 us
    add x14, other arithmetic, body(): lax.associative_scan(combine_link, (decays, driving), axis=0)  25 us
    reduce_scatter x1, waiting for transfers between devices, body(): lax.psum_scatter(partial_out.astype(jnp.bfloat16), 'ctx', scatter_dimensi...  25 us
  transfers between devices with their start and end apart: 4, of which 4 were waited for; matrix products, arithmetic and copies ran while one was open for 0% of the time, Pallas kernels for 0%

commit v1 on v0

--- a/solution.py
+++ b/solution.py
@@ -1,6 +1,8 @@
 import jax
 import jax.numpy as jnp
 from jax import lax
+from jax.experimental import pallas as pl
+from jax.experimental.pallas import tpu as pltpu
 from jax.sharding import PartitionSpec as P
 
 
@@ -41,6 +43,106 @@
 
 def combine_link(earlier, later_link):
     return (earlier[0] * later_link[0], later_link[0] * earlier[1] + later_link[1])
+
+
+def fold_states(rates, states, step, drive, in_ref, t):
+    return tuple(
+        jnp.exp(step * rate) * state + drive * in_ref[n, t]
+        for n, (rate, state) in enumerate(zip(rates, states))
+    )
+
+
+def end_kernel(step_ref, drive_ref, rate_ref, in_ref, end_ref):
+    count = rate_ref.shape[0]
+    rates = [rate_ref[n] for n in range(count)]
+
+    def advance(t, carried):
+        states, total = carried
+        step = step_ref[t]
+        return (fold_states(rates, states, step, drive_ref[t], in_ref, t), total + step)
+
+    zero = jnp.zeros(rate_ref.shape[1:], jnp.float32)
+    states, total = lax.fori_loop(
+        0, step_ref.shape[0], advance, ((zero,) * count, zero), unroll=4
+    )
+    for n in range(count):
+        end_ref[n] = states[n]
+    end_ref[count] = total
+
+
+def read_kernel(
+    step_ref, drive_ref, signal_ref, gate_ref, skip_ref, rate_ref, ends_ref, in_ref, out_ref, res_ref
+):
+    count = rate_ref.shape[0]
+    mine = lax.axis_index("ctx")
+    rates = [rate_ref[n] for n in range(count)]
+    zero = jnp.zeros(rate_ref.shape[1:], jnp.float32)
+
+    def join(block, states):
+        total = ends_ref[block, count]
+        return tuple(
+            jnp.exp(total * rates[n]) * states[n] + ends_ref[block, n] for n in range(count)
+        )
+
+    incoming = lax.fori_loop(0, mine, join, (zero,) * count)
+    skip = skip_ref[...]
+
+    def advance(t, states):
+        states = fold_states(rates, states, step_ref[t], drive_ref[t], in_ref, t)
+        terms = [states[n] * out_ref[n, t] for n in range(count)]
+        while len(terms) > 1:
+            terms = [terms[i] + terms[i + 1] for i in range(0, len(terms), 2)]
+        gate = gate_ref[t]
+        res_ref[t] = (terms[0] + skip * signal_ref[t]) * (gate / (1.0 + jnp.exp(-gate)))
+        return states
+
+    lax.fori_loop(0, step_ref.shape[0], advance, incoming, unroll=4)
+
+
+def scanned(mamba_in, gate_in, step_size, input_proj, output_proj, decay_log, skip_gain):
+    length, channels = mamba_in.shape
+    count = decay_log.shape[0]
+    tile = (channels // 128, 128)
+    signal = mamba_in.astype(jnp.float32).reshape((length,) + tile)
+    gate = gate_in.astype(jnp.float32).reshape((length,) + tile)
+    step = step_size.reshape((length,) + tile)
+    drive = step * signal
+    rate = -jnp.exp(decay_log).reshape((count,) + tile)
+    vmem = pl.BlockSpec(memory_space=pltpu.VMEM)
+    smem = pl.BlockSpec(memory_space=pltpu.SMEM)
+    ends = pl.pallas_call(
+        end_kernel,
+        out_shape=jax.ShapeDtypeStruct((count + 1,) + tile, jnp.float32),
+        in_specs=[vmem] * 3 + [smem],
+        out_specs=vmem,
+        name="end_states",
+    )(step, drive, rate, input_proj)
+    ends = lax.all_gather(ends, "ctx")
+    gated = pl.pallas_call(
+        read_kernel,
+        out_shape=jax.ShapeDtypeStruct((length,) + tile, jnp.float32),
+        in_specs=[vmem] * 7 + [smem] * 2,
+        out_specs=vmem,
+        name="read_states",
+    )(step, drive, signal, gate, skip_gain.reshape(tile), rate, ends, input_proj, output_proj)
+    return gated.reshape(length, channels).astype(jnp.bfloat16)
+
+
+def scanned_small(mamba_in, gate_in, step_size, input_proj, output_proj, decay_log, skip_gain):
+    decay_rate = -jnp.exp(decay_log)
+    signal = mamba_in.astype(jnp.float32)
+    decays = jnp.exp(step_size[:, None, :] * decay_rate[None, :, :])
+    driving = (step_size * signal)[:, None, :] * jnp.transpose(input_proj)[:, :, None]
+    cum_decay, local_state = lax.associative_scan(combine_link, (decays, driving), axis=0)
+    summary = (cum_decay[-1], local_state[-1])
+    identity = (jnp.ones_like(summary[0]), jnp.zeros_like(summary[1]))
+    prefix = prefix_2(summary, "ctx", combine_link, identity)
+    incoming = prefix[1]
+    full_state = local_state + cum_decay * incoming[None, :, :]
+    readout = jnp.sum(jnp.transpose(output_proj)[:, :, None] * full_state, axis=1)
+    return ((readout + skip_gain * signal) * jax.nn.silu(gate_in.astype(jnp.float32))).astype(
+        jnp.bfloat16
+    )
 
 
 def body(
@@ -59,20 +161,10 @@
     w_up,
     w_down,
 ):
-    length = mamba_in.shape[0]
-    decay_rate = -jnp.exp(decay_log)
-    signal = mamba_in.astype(jnp.float32)
-    decays = jnp.exp(step_size[:, None, :] * decay_rate[None, :, :])
-    driving = (step_size * signal)[:, None, :] * jnp.transpose(input_proj)[:, :, None]
-    cum_decay, local_state = lax.associative_scan(combine_link, (decays, driving), axis=0)
-    summary = (cum_decay[-1], local_state[-1])
-    identity = (jnp.ones_like(summary[0]), jnp.zeros_like(summary[1]))
-    prefix = prefix_2(summary, "ctx", combine_link, identity)
-    incoming = prefix[1]
-    full_state = local_state + cum_decay * incoming[None, :, :]
-    readout = jnp.sum(jnp.transpose(output_proj)[:, :, None] * full_state, axis=1)
-    gated_out = ((readout + skip_gain * signal) * jax.nn.silu(gate_in.astype(jnp.float32))).astype(
-        jnp.bfloat16
+    length, channels = mamba_in.shape
+    scan = scanned if channels % 128 == 0 else scanned_small
+    gated_out = scan(
+        mamba_in, gate_in, step_size, input_proj, output_proj, decay_log, skip_gain
     )
     experts = lax.axis_size("exp")
     top_count = routes.shape[1]

time: 646 us -> 271 us (0.42); the launches traced: 633 us -> 271 us
  local copies, waits for them, and re-layouts: 268 us -> 4.65 us
  other arithmetic: 111 us -> 7.7 us
  Pallas kernels: 0 us -> 9.89 us
    pad x24 -> x0, local copies, waits for them, and re-layouts: 255 us -> none  [body(): lax.associative_scan(combine_link, (decays, driving), axis=0)]
    add x26 -> x0, other arithmetic: 63.1 us -> none  [the longest x12 38.1 us: combine_link(): later_link[0] * earlier[1] + later_link[1]]
    concatenate x12 -> x0, other arithmetic: 20.5 us -> none  [body(): lax.associative_scan(combine_link, (decays, driving), axis=0)]
    reduce_sum x1 -> x0, other arithmetic: 13.9 us -> none  [body(): jnp.sum(jnp.transpose(output_proj)[:, :, None] * full_state, axis=1)]
    pallas_call x0 -> x2, Pallas kernels: none -> 9.89 us  [the longest x1 5.87 us: scanned(): pl.pallas_call(read_kernel, out_shape=jax.ShapeDtypeStruct((length,) + ti...]
    exp x1 -> x0, other arithmetic: 7.58 us -> none  [body(): decays = jnp.exp(step_size[:, None, :] * decay_rate[None, :, :])]
    all_gather x2 -> x1, blocking collectives: 13.1 us -> 8.88 us  [scanned(): ends = lax.all_gather(ends, 'ctx')]
  transfers between devices with their start and end apart: 4 -> 4, of which waited for: 4 -> 4; matrix products, arithmetic and copies ran while one was open for 0% -> 1% of each run, Pallas kernels for 0% -> 0%
where the time goes in v1:
time: 271 us
  waiting for transfers between devices  165 us (61%)
  blocking collectives  40.4 us (15%)
  matrix products  29.2 us (11%)
  between operations  13.3 us (5%)
  Pallas kernels  9.89 us (4%)
  other arithmetic  7.7 us (3%)
  local copies, waits for them, and re-layouts  4.65 us (2%)
    reduce_scatter x1, waiting for transfers between devices, body(): lax.psum_scatter(mixed_rows + lax.dynamic_update_slice_in_dim(placed, lif...  62.6 us
    all_gather x1, waiting for transfers between devices, body(): lax.all_gather(hidden, 'tp', axis=1, tiled=True)  50.9 us
    all_gather x1, blocking collectives, body(): lax.all_gather(rms_scale(token_part, norm_gain), ('exp', 'tp'), axis=0, t...  31.5 us
    all_gather x1, waiting for transfers between devices, body(): row_block = lax.all_gather(normed, ('ctx', 'tp'), axis=0, tiled=True)  26.8 us
    reduce_scatter x1, waiting for transfers between devices, body(): lax.psum_scatter(partial_out.astype(jnp.bfloat16), 'ctx', scatter_dimensi...  25 us
    dot_general x1, matrix products, body(): jnp.dot(lax.all_gather(hidden, 'tp', axis=1, tiled=True), local_down, pre...  9.11 us
    all_gather x1, blocking collectives, scanned(): ends = lax.all_gather(ends, 'ctx')  8.88 us
    dot_general x1, matrix products, body(): up_part = jnp.dot(row_block, w_up[0], preferred_element_type=jnp.float32)  8.43 us
  transfers between devices with their start and end apart: 4, of which 4 were waited for; matrix products, arithmetic and copies ran while one was open for 1% of the time, Pallas kernels for 0%

profile of v1, /device:TPU:0, one launch (start us, length us, event | category | flops | bytes accessed | tf_op | source)
XLA Modules:
  0.0 270.6 jit_solution(12815064621940076834)
XLA Ops:
  6.5 0.0 reduce-scatter.3.cloned.1.call-start
  6.5 0.9 negate_bitcast_fusion
  7.4 0.6 copy.46
  8.1 1.1 copy.43
  9.2 0.0 copy-start
  9.2 1.2 convert_bitcast_fusion.1
  10.4 0.1 copy.44
  10.5 0.0 copy-start.2
  10.5 1.0 bitcast_multiply_fusion.drive_ref
  11.5 4.0 %end_states.1 = f32[17,8,128]{2,1,0:T(8,128)} custom-call(f32[128,8,128]{2,1,0:T(8,128)} %bitcast.58, f32[128,8,128]{2,1,0:T(8,128)} %bitcast_multiply_fusion.drive_ref, f32[16,8,128]{2,1,0:T(8,128)} %bitcast.64, f32[16,128]{1,0:T(8,128)} %in_ref.3), custom_call_target="tpu_custom_call" | custom-call | tf_op jit(solution)/shard_map/end_states/pallas_call | solution.py:113
  15.5 8.9 %all-gather = f32[68,8,128]{2,1,0:T(8,128)} all-gather(f32[17,8,128]{2,1,0:T(8,128)} %end_states.1), channel_id=2, replica_groups=mesh['ctx'=4,'exp'=4,'tp'=2] {'ctx'}, dimensions={0}, use_global_device_ids=true | all-gather | bytes 348160 | tf_op jit(solution)/shard_map/all_gather | solution.py:120
  24.4 0.9 copy.45
  25.4 5.9 %read_states.1 = f32[128,8,128]{2,1,0:T(8,128)} custom-call(f32[128,8,128]{2,1,0:T(8,128)} %bitcast.59, f32[128,8,128]{2,1,0:T(8,128)} %bitcast_multiply_fusion.drive_ref, f32[128,8,128]{2,1,0:T(8,128)} %bitcast.60, f32[128,8,128]{2,1,0:T(8,128)} %bitcast.61, f32[8,128]{1,0:T(8,128)} %bitcast.67, f32[16,8,128]{2,1,0:T(8,128)} %bitcast.65, ...), custom_call_target="tpu_custom_call" | custom-call | tf_op jit(solution)/shard_map/read_states/pallas_call | solution.py:121
  31.2 1.1 convert_element_type.40
  32.3 0.0 copy-start.5
  32.3 2.9 %fusion.11 = f32[128,2048]{1,0:T(8,128)S(1)} fusion(bf16[1024,2048]{1,0:T(8,128)(2,1)} %param.21, bf16[16,8,8,128]{3,2,1,0:T(8,128)(2,1)S(1)} %bitcast.63), kind=kOutput, calls=%fused_computation.11 | convolution fusion | flops 536870912 | bytes 5505024 | tf_op jit(solution)/shard_map/dot_general | solution.py:177
  35.3 0.0 copy-done.4
  35.3 1.0 copy-done.1
  36.3 0.0 reduce-scatter.3.cloned.1.call-update
  36.3 0.0 all-gather.4.cloned.1.call-start
  36.4 0.1 copy.37
  36.5 0.1 eq.42
  36.6 0.1 eq.38
  36.8 1.2 reduce-window.6
  38.0 0.1 slice.8
  38.1 0.1 copy.39
  38.2 0.1 copy.40
  38.3 0.1 add_bitcast_fusion
  38.4 0.1 reduce_sum.30
  38.6 0.1 copy.41
  38.6 0.1 convert_reduce_fusion
  38.8 62.6 %reduce-scatter.3.cloned.1.call-done = f32[16,2048]{1,0:T(8,128)} async-done(((f32[128,2048]{1,0:T(8,128)}), f32[16,2048]{1,0:T(8,128)}) %reduce-scatter.3.cloned.1.call-update) | async-done | bytes 131088 | tf_op jit(solution)/shard_map/reduce_scatter | solution.py:180
  101.4 1.0 multiply_reduce_fusion
  102.4 0.0 copy-done.5
  102.4 1.0 multiply_convert_fusion.1
  103.4 31.5 %all_gather.17 = bf16[128,2048]{1,0:T(8,128)(2,1)S(1)} all-gather(bf16[16,2048]{1,0:T(8,128)(2,1)S(1)} %multiply_convert_fusion.1), channel_id=1, replica_groups=mesh['ctx'=4,'exp'=4,'tp'=2] {'exp','tp'}, dimensions={0}, use_global_device_ids=true | all-gather | bytes 589824 | tf_op jit(solution)/shard_map/all_gather | solution.py:186
  134.9 0.9 convolution_convert_fusion
  135.9 0.0 all-gather.4.cloned.1.call-update
  135.9 0.0 all-gather.6.cloned.1.call-start
  135.9 26.8 %all-gather.4.cloned.1.call-done = bf16[512,2048]{1,0:T(8,128)(2,1)} async-done(((bf16[64,2048]{1,0:T(8,128)(2,1)}), bf16[512,2048]{1,0:T(8,128)(2,1)}) %all-gather.4.cloned.1.call-update) | async-done | bytes 2097168 | tf_op jit(solution)/shard_map/all_gather | solution.py:191
  162.7 7.8 %fusion.4 = f32[512,1792]{1,0:T(8,128)S(1)} fusion(bf16[512,2048]{1,0:T(8,128)(2,1)} %all-gather.4.cloned.1.call-done, bf16[1,2048,1792]{2,1,0:T(8,128)(2,1)} %param.25), kind=kOutput, calls=%fused_computation.4 | convolution fusion | flops 3758096384 | bytes 13107200 | tf_op jit(solution)/shard_map/dot_general | solution.py:192
  170.5 8.4 %multiply_convert_fusion = bf16[512,1792]{1,0:T(8,128)(2,1)} fusion(f32[512,1792]{1,0:T(8,128)S(1)} %fusion.4, bf16[512,2048]{1,0:T(8,128)(2,1)S(1)} %copy-done.7, bf16[1,2048,1792]{2,1,0:T(8,128)(2,1)} %param.26), kind=kOutput, calls=%fused_computation.6 | convolution fusion | flops 3763601408 | bytes 14942208 | tf_op jit(solution)/shard_map/dot_general | solution.py:193
  179.0 0.0 all-gather.6.cloned.1.call-update
  179.0 0.0 reduce-scatter.5.cloned.1.call-start
  179.0 50.9 %all-gather.6.cloned.1.call-done = bf16[512,3584]{1,0:T(8,128)(2,1)} async-done(((bf16[512,1792]{1,0:T(8,128)(2,1)}), bf16[512,3584]{1,0:T(8,128)(2,1)}) %all-gather.6.cloned.1.call-update) | async-done | bytes 3670032 | tf_op jit(solution)/shard_map/all_gather | solution.py:197
  229.9 9.1 %fusion.8 = bf16[512,1024]{1,0:T(8,128)(2,1)} fusion(bf16[512,3584]{1,0:T(8,128)(2,1)} %all-gather.6.cloned.1.call-done, bf16[1,3584,1024]{2,1,0:T(8,128)(2,1)} %param.27), kind=kOutput, calls=%fused_computation.8 | convolution fusion | flops 3758620672 | bytes 12058624 | tf_op jit(solution)/shard_map/dot_general | solution.py:196
  239.1 0.0 reduce-scatter.5.cloned.1.call-update
  239.1 25.0 %reduce-scatter.5.cloned.1.call-done = bf16[128,1024]{1,0:T(8,128)(2,1)} async-done(((bf16[512,1024]{1,0:T(8,128)(2,1)}), bf16[128,1024]{1,0:T(8,128)(2,1)}) %reduce-scatter.5.cloned.1.call-update) | async-done | bytes 262160 | tf_op jit(solution)/shard_map/reduce_scatter | solution.py:201
  (19 shorter events, 0.2 us)
Async XLA Ops:
  6.5 17.9 %copy-start.3 = (bf16[128,1024]{1,0:T(8,128)(2,1)S(1)}, bf16[128,1024]{1,0:T(8,128)(2,1)}, u32[]{:S(2)}) copy-start(bf16[128,1024]{1,0:T(8,128)(2,1)} %param.15) | copy-start | bytes 786436
  6.5 94.8 %reduce-scatter.3.cloned.1.call-start = ((), (), s32[]{:S(2)}) async-start(), calls=%async_computation.2 | async-start | bytes 1179648 | tf_op jit(solution)/shard_map/reduce_scatter | solution.py:180
  9.2 2.3 copy-start
  10.5 14.8 %copy-start.2 = (f32[16,8,8,128]{3,2,1,0:T(8,128)}, f32[16,8,8,128]{3,2,1,0:T(8,128)S(1)}, u32[]{:S(2)}) copy-start(f32[16,8,8,128]{3,2,1,0:T(8,128)S(1)} %copy.44) | copy-start | bytes 1572868
  31.2 4.0 %copy-start.4 = (bf16[128,256]{1,0:T(8,128)(2,1)S(1)}, bf16[128,256]{1,0:T(8,128)(2,1)}, u32[]{:S(2)}) copy-start(bf16[128,256]{1,0:T(8,128)(2,1)} %param.22) | copy-start | bytes 196612
  31.2 5.1 %copy-start.6 = (s32[128,2]{0,1:T(2,128)S(1)}, s32[128,2]{0,1:T(2,128)}, u32[]{:S(2)}) copy-start(s32[128,2]{0,1:T(2,128)} %param.23) | copy-start | bytes 3076
  32.3 70.1 %copy-start.5 = (f32[2048]{0:T(1024)S(1)}, f32[2048]{0:T(1024)}, u32[]{:S(2)}) copy-start(f32[2048]{0:T(1024)} %param.24) | copy-start | bytes 24580
  35.3 1.0 copy-start.1
  36.3 126.4 %all-gather.4.cloned.1.call-start = ((), (), s32[]{:S(2)}) async-start(), calls=%async_computation.3 | async-start | bytes 2359296 | tf_op jit(solution)/shard_map/all_gather | solution.py:191
  135.9 94.0 %all-gather.6.cloned.1.call-start = ((), (), s32[]{:S(2)}) async-start(), calls=%async_computation.4 | async-start | bytes 5505024 | tf_op jit(solution)/shard_map/all_gather | solution.py:197
  162.7 7.8 %copy-start.7 = (bf16[512,2048]{1,0:T(8,128)(2,1)S(1)}, bf16[512,2048]{1,0:T(8,128)(2,1)}, u32[]{:S(2)}) copy-start(bf16[512,2048]{1,0:T(8,128)(2,1)} %all-gather.4.cloned.1.call-done) | copy-start | bytes 6291460
  179.0 85.1 %reduce-scatter.5.cloned.1.call-start = ((), (), s32[]{:S(2)}) async-start(), calls=%async_computation.5 | async-start | bytes 1310720 | tf_op jit(solution)/shard_map/reduce_scatter | solution.py:201
Sparse Core Ops, SparseCore 0:
  36.4 64.8 reduce-scatter.2
  136.0 26.6 all-gather.3
  179.1 50.7 all-gather.5
  239.2 24.8 reduce-scatter.4

commit v2 on v1

--- a/solution.py
+++ b/solution.py
@@ -128,6 +128,347 @@
     return gated.reshape(length, channels).astype(jnp.bfloat16)
 
 
+MESH = pl.DeviceIdType.MESH
+
+
+def greet(peers):
+    barrier = pltpu.get_barrier_semaphore()
+    for peer in peers:
+        pl.semaphore_signal(barrier, inc=1, device_id=peer, device_id_type=MESH)
+    pl.semaphore_wait(barrier, len(peers))
+
+
+def expert_steps(rows_ref, out_ref, weights, wd_copy, bufs, sems):
+    wg, wu, wd, gate_copy, up_copy = weights
+    own, other, acc, part, inbox = bufs
+    h_send, h_recv, r_send, r_recv = sems
+    ctx, tp = lax.axis_index("ctx"), lax.axis_index("tp")
+    blocks, capacity, depth = rows_ref.shape
+    chunks, tiles, _, width = own.shape
+    piece = capacity // chunks
+
+    def hidden_copy(j, k):
+        return pltpu.make_async_remote_copy(
+            src_ref=own.at[j, k],
+            dst_ref=other.at[j, k],
+            send_sem=h_send.at[j, k],
+            recv_sem=h_recv.at[j, k],
+            device_id={"tp": 1 - tp},
+            device_id_type=MESH,
+        )
+
+    def part_copy(j, d):
+        target = lax.rem(ctx + d, blocks)
+        return pltpu.make_async_remote_copy(
+            src_ref=part.at[j, target],
+            dst_ref=inbox.at[j, d - 1],
+            send_sem=r_send.at[j, d - 1],
+            recv_sem=r_recv.at[j, d - 1],
+            device_id={"ctx": target},
+            device_id_type=MESH,
+        )
+
+    for j in range(chunks):
+
+        def hidden_step(k, unused, j=j):
+            if j == 0:
+                gate_copy(k).wait()
+                up_copy(k).wait()
+            rows = rows_ref[:, pl.ds(j * piece, piece), :].reshape(blocks * piece, depth)
+            gate = jnp.dot(rows, wg[k], preferred_element_type=jnp.float32)
+            up = jnp.dot(rows, wu[k], preferred_element_type=jnp.float32)
+            own[j, k] = (gate / (1.0 + jnp.exp(-gate)) * up).astype(jnp.bfloat16)
+            hidden_copy(j, k).start()
+            return unused
+
+        lax.fori_loop(0, tiles, hidden_step, 0)
+    wd_copy().wait()
+    for j in range(chunks):
+        acc[...] = jnp.zeros_like(acc)
+
+        def down_step(k, unused, j=j):
+            mine = pl.multiple_of((tp * tiles + k) * width, width)
+            acc[...] += jnp.dot(
+                own[j, k], wd[pl.ds(mine, width), :], preferred_element_type=jnp.float32
+            )
+            return unused
+
+        def down_step_other(k, unused, j=j):
+            hidden_copy(j, k).wait_recv()
+            theirs = pl.multiple_of(((1 - tp) * tiles + k) * width, width)
+            acc[...] += jnp.dot(
+                other[j, k], wd[pl.ds(theirs, width), :], preferred_element_type=jnp.float32
+            )
+            return unused
+
+        lax.fori_loop(0, tiles, down_step, 0)
+        lax.fori_loop(0, tiles, down_step_other, 0)
+        part[j] = acc[...].reshape(blocks, piece, acc.shape[1]).astype(jnp.bfloat16)
+        for d in range(1, blocks):
+            part_copy(j, d).start()
+    for j in range(chunks):
+        total = part[j, ctx].astype(jnp.float32)
+        for d in range(1, blocks):
+            part_copy(j, d).wait_recv()
+            total = total + inbox[j, d - 1].astype(jnp.float32)
+        out_ref[pl.ds(j * piece, piece), :] = total.astype(out_ref.dtype)
+
+    def drain(k, unused):
+        for j in range(chunks):
+            hidden_copy(j, k).wait_send()
+        return unused
+
+    lax.fori_loop(0, tiles, drain, 0)
+    for j in range(chunks):
+        for d in range(1, blocks):
+            part_copy(j, d).wait_send()
+
+
+def weight_copies(gate_hbm, up_hbm, down_hbm, wg, wu, wd, g_sem, u_sem, d_sem):
+    width = wg.shape[2]
+
+    def columns(k):
+        return pl.ds(pl.multiple_of(k * width, width), width)
+
+    def gate_copy(k):
+        return pltpu.make_async_copy(gate_hbm.at[:, columns(k)], wg.at[k], g_sem.at[k])
+
+    def up_copy(k):
+        return pltpu.make_async_copy(up_hbm.at[:, columns(k)], wu.at[k], u_sem.at[k])
+
+    def wd_copy():
+        return pltpu.make_async_copy(down_hbm, wd, d_sem)
+
+    return gate_copy, up_copy, wd_copy
+
+
+def expert_kernel(
+    rows_ref, gate_hbm, up_hbm, down_hbm, out_ref,
+    wg, wu, wd, own, other, acc, part, inbox,
+    g_sem, u_sem, d_sem, h_send, h_recv, r_send, r_recv,
+):
+    gate_copy, up_copy, wd_copy = weight_copies(
+        gate_hbm, up_hbm, down_hbm, wg, wu, wd, g_sem, u_sem, d_sem
+    )
+    for k in range(wg.shape[0]):
+        gate_copy(k).start()
+        up_copy(k).start()
+    wd_copy().start()
+    ctx, tp = lax.axis_index("ctx"), lax.axis_index("tp")
+    blocks = rows_ref.shape[0]
+    greet([{"tp": 1 - tp}] + [{"ctx": lax.rem(ctx + d, blocks)} for d in range(1, blocks)])
+    expert_steps(
+        rows_ref, out_ref, (wg, wu, wd, gate_copy, up_copy), wd_copy,
+        (own, other, acc, part, inbox), (h_send, h_recv, r_send, r_recv),
+    )
+
+
+def expert_scratch(blocks, capacity, depth, hidden, out_width):
+    chunks, width = 4, 256
+    tiles = hidden // width
+    piece = capacity // chunks
+    bf16, dma = jnp.bfloat16, pltpu.SemaphoreType.DMA
+    return [
+        pltpu.VMEM((tiles, depth, width), bf16),
+        pltpu.VMEM((tiles, depth, width), bf16),
+        pltpu.VMEM((2 * hidden, out_width), bf16),
+        pltpu.VMEM((chunks, tiles, blocks * piece, width), bf16),
+        pltpu.VMEM((chunks, tiles, blocks * piece, width), bf16),
+        pltpu.VMEM((blocks * piece, out_width), jnp.float32),
+        pltpu.VMEM((chunks, blocks, piece, out_width), bf16),
+        pltpu.VMEM((chunks, blocks - 1, piece, out_width), bf16),
+        dma((tiles,)),
+        dma((tiles,)),
+        dma,
+        dma((chunks, tiles)),
+        dma((chunks, tiles)),
+        dma((chunks, blocks - 1)),
+        dma((chunks, blocks - 1)),
+    ]
+
+
+def experts_tiled(row_block, w_gate, w_up, w_down):
+    blocks, capacity, depth = row_block.shape
+    vmem, anywhere = pl.BlockSpec(memory_space=pltpu.VMEM), pl.BlockSpec(memory_space=pl.ANY)
+    return pl.pallas_call(
+        expert_kernel,
+        out_shape=jax.ShapeDtypeStruct((capacity, w_down.shape[1]), jnp.bfloat16),
+        in_specs=[vmem] + [anywhere] * 3,
+        out_specs=vmem,
+        scratch_shapes=expert_scratch(
+            blocks, capacity, depth, w_gate.shape[1], w_down.shape[1]
+        ),
+        compiler_params=pltpu.CompilerParams(
+            collective_id=0, has_side_effects=True, vmem_limit_bytes=60 << 20
+        ),
+        name="experts",
+    )(row_block, w_gate, w_up, w_down)
+
+
+def mix_kernel(
+    gated_ref, weight_ref, residual_ref, gain_ref, pick_ref, rows_ref,
+    mix, inbox, tokens, picks,
+    p_send, p_recv, m_send, m_recv, a_send, a_recv, c_send, c_recv,
+):
+    ctx, exp, tp = lax.axis_index("ctx"), lax.axis_index("exp"), lax.axis_index("tp")
+    blocks, experts = lax.axis_size("ctx"), lax.axis_size("exp")
+    group = 2 * experts
+    place = exp * 2 + tp
+    shard, depth = mix.shape[1:]
+    width = residual_ref.shape[1]
+    across = lax.rem(ctx + 2, blocks)
+    partner = ctx + 1 - 2 * lax.rem(ctx, 2)
+    line = ctx * 2 + tp
+
+    def member(d):
+        other = lax.rem(place + d, group)
+        return other, {"exp": other // 2, "tp": lax.rem(other, 2)}
+
+    greet(
+        [member(d)[1] for d in range(1, group)]
+        + [{"ctx": lax.rem(ctx + d, blocks)} for d in range(1, blocks)]
+    )
+
+    def send(src, dst, send_sem, recv_sem, device):
+        return pltpu.make_async_remote_copy(
+            src_ref=src, dst_ref=dst, send_sem=send_sem, recv_sem=recv_sem,
+            device_id=device, device_id_type=MESH,
+        )
+
+    pick_copies = [
+        send(
+            pick_ref, picks.at[ctx], p_send.at[d - 1], p_recv.at[d - 1],
+            {"ctx": lax.rem(ctx + d, blocks)},
+        )
+        for d in range(1, blocks)
+    ]
+    for copy in pick_copies:
+        copy.start()
+    picks[ctx] = pick_ref[...]
+
+    lifted = residual_ref[...].astype(jnp.float32)
+    for n in range(group):
+        columns = slice(n * width, (n + 1) * width)
+        mixed = jnp.dot(
+            gated_ref[...], weight_ref[:, columns], preferred_element_type=jnp.float32
+        )
+        mixed = mixed + jnp.where(place == n, lifted, 0.0)
+        mix[:, :, columns] = mixed.astype(jnp.bfloat16).reshape(group, shard, width)
+    mix_copies = []
+    for d in range(1, group):
+        other, device = member(d)
+        mix_copies.append(
+            send(mix.at[other], inbox.at[d - 1], m_send.at[d - 1], m_recv.at[d - 1], device)
+        )
+    for copy in mix_copies:
+        copy.start()
+    total = mix[place].astype(jnp.float32)
+    for d in range(1, group):
+        mix_copies[d - 1].wait_recv()
+        total = total + inbox[d - 1].astype(jnp.float32)
+    mean_sq = jnp.mean(total * total, axis=1, keepdims=True)
+    tokens[line, exp] = (total * lax.rsqrt(mean_sq + 1e-06) * gain_ref[...]).astype(jnp.bfloat16)
+
+    def spread(kind, d, which, device):
+        owner = lax.rem(exp - d + experts, experts)
+        here = tokens.at[which, owner]
+        return send(here, here, a_send.at[kind, d], a_recv.at[kind, d], device)
+
+    def share(kind, d, which):
+        owner = lax.rem(exp - d + experts, experts)
+        here = tokens.at[which, owner]
+        return send(here, here, c_send.at[kind, d], c_recv.at[kind, d], {"ctx": partner})
+
+    started, landed = [], []
+    mine = tokens.at[line, exp]
+    depth_copies = [
+        send(
+            mine, mine, a_send.at[0, d], a_recv.at[0, d],
+            {"exp": lax.rem(exp + d, experts)},
+        )
+        for d in range(1, experts)
+    ]
+    for copy in depth_copies:
+        copy.start()
+    started += depth_copies
+    line_y = ctx * 2 + 1 - tp
+    line_x = across * 2 + tp
+    line_xy = across * 2 + 1 - tp
+    over_y, over_x, over_xy = [], [], []
+    for d in range(experts):
+        if d > 0:
+            depth_copies[d - 1].wait_recv()
+        over_y.append(spread(1, d, line, {"tp": 1 - tp}))
+        over_x.append(spread(2, d, line, {"ctx": across}))
+        near = share(0, d, line)
+        for copy in (over_y[d], over_x[d], near):
+            copy.start()
+        landed.append(near)
+    for d in range(experts):
+        over_y[d].wait_recv()
+        over_xy.append(spread(3, d, line_y, {"ctx": across}))
+        near = share(1, d, line_y)
+        for copy in (over_xy[d], near):
+            copy.start()
+        landed.append(near)
+        over_x[d].wait_recv()
+        near = share(2, d, line_x)
+        near.start()
+        landed.append(near)
+    for d in range(experts):
+        over_xy[d].wait_recv()
+        near = share(3, d, line_xy)
+        near.start()
+        landed.append(near)
+    for copy in landed:
+        copy.wait_recv()
+    for copy in pick_copies:
+        copy.wait_recv()
+    for block in range(blocks):
+        rows_ref[block] = jnp.dot(
+            picks[block],
+            tokens[2 * block : 2 * block + 2].reshape(group * shard, depth),
+            preferred_element_type=jnp.float32,
+        ).astype(jnp.bfloat16)
+    for copy in started + over_y + over_x + over_xy + landed + mix_copies + pick_copies:
+        copy.wait_send()
+
+
+def mixed_slots(gated_out, out_weight, residual, norm_gain, row_ids, capacity):
+    blocks, experts = lax.axis_size("ctx"), lax.axis_size("exp")
+    length, depth = gated_out.shape[0], out_weight.shape[1]
+    group = 2 * experts
+    shard = length // group
+    pick = pick_rows(row_ids, lax.axis_index("exp") * capacity, capacity)
+    pick = pick.reshape(capacity, experts, 2, shard).transpose(0, 2, 1, 3)
+    bf16, dma = jnp.bfloat16, pltpu.SemaphoreType.DMA
+    vmem = pl.BlockSpec(memory_space=pltpu.VMEM)
+    return pl.pallas_call(
+        mix_kernel,
+        out_shape=jax.ShapeDtypeStruct((blocks, capacity, depth), bf16),
+        in_specs=[vmem] * 5,
+        out_specs=vmem,
+        scratch_shapes=[
+            pltpu.VMEM((group, shard, depth), bf16),
+            pltpu.VMEM((group - 1, shard, depth), bf16),
+            pltpu.VMEM((2 * blocks, experts, shard, depth), bf16),
+            pltpu.VMEM((blocks, capacity, length), bf16),
+            dma((blocks - 1,)),
+            dma((blocks - 1,)),
+            dma((group - 1,)),
+            dma((group - 1,)),
+            dma((4, experts)),
+            dma((4, experts)),
+            dma((4, experts)),
+            dma((4, experts)),
+        ],
+        compiler_params=pltpu.CompilerParams(
+            collective_id=1, has_side_effects=True, vmem_limit_bytes=40 << 20
+        ),
+        name="mix",
+    )(gated_out, out_weight, residual, norm_gain[None, :], pick.reshape(capacity, length))
+
+
 def scanned_small(mamba_in, gate_in, step_size, input_proj, output_proj, decay_log, skip_gain):
     decay_rate = -jnp.exp(decay_log)
     signal = mamba_in.astype(jnp.float32)
@@ -170,6 +511,17 @@
     top_count = routes.shape[1]
     capacity = length * top_count * 2 // experts
     row_ids = route_rows(routes, capacity, experts)
+    shard = length // (experts * lax.axis_size("tp"))
+    if (
+        lax.axis_size("tp") == 2
+        and lax.axis_size("ctx") == 4
+        and residual.shape[1] % 128 == 0
+        and w_gate.shape[2] % 256 == 0
+        and capacity % 64 == 0
+        and shard % 16 == 0
+    ):
+        slots = mixed_slots(gated_out, out_weight, residual, norm_gain, row_ids, capacity)
+        return experts_tiled(slots, w_gate[0], w_up[0], w_down[0])[None, None]
     rows_here = capacity // lax.axis_size("tp")
     col_width = residual.shape[1]
     model_width = out_weight.shape[1]

time: 271 us -> 123 us (0.45)
  waiting for transfers between devices: 165 us -> 0 us
  Pallas kernels: 9.89 us -> 97.1 us
  blocking collectives: 40.4 us -> 8.89 us
  matrix products: 29.2 us -> 0 us
  between operations: 13.3 us -> 0.18 us
  local copies, waits for them, and re-layouts: 4.65 us -> 9.32 us
    reduce_scatter x2 -> x0, waiting for transfers between devices: 87.6 us -> none  [the longest x1 62.6 us: body(): lax.psum_scatter(mixed_rows + lax.dynamic_update_slice_in_dim(placed, lif...]
    pallas_call x0 -> x2, Pallas kernels: none -> 87.3 us  [the longest x1 51.4 us: experts_tiled(): pl.pallas_call(expert_kernel, out_shape=jax.ShapeDtypeStruct((capacity, w...]
    all_gather x2 -> x0, waiting for transfers between devices: 77.7 us -> none  [the longest x1 50.9 us: body(): lax.all_gather(hidden, 'tp', axis=1, tiled=True)]
    all_gather x1 -> x0, blocking collectives: 31.5 us -> none  [body(): lax.all_gather(rms_scale(token_part, norm_gain), ('exp', 'tp'), axis=0, t...]
    dot_general x5 -> x0, matrix products: 29.2 us -> none  [the longest x1 9.11 us: body(): jnp.dot(lax.all_gather(hidden, 'tp', axis=1, tiled=True), local_down, pre...]
    unnamed x21, local copies, waits for them, and re-layouts: 3.9 us -> 8.34 us
  transfers between devices with their start and end apart: 4 -> 0, of which waited for: 4 -> 0; matrix products, arithmetic and copies ran while one was open for 1% -> 0% of each run, Pallas kernels for 0% -> 0%
where the time goes in v2:
time: 123 us; the launch traced here: 122 us
  Pallas kernels  97.1 us (79%)
  local copies, waits for them, and re-layouts  9.32 us (8%)
  blocking collectives  8.89 us (7%)
  other arithmetic  6.34 us (5%)
    pallas_call x1, Pallas kernels, experts_tiled(): pl.pallas_call(expert_kernel, out_shape=jax.ShapeDtypeStruct((capacity, w...  51.4 us
    pallas_call x1, Pallas kernels, mixed_slots(): pl.pallas_call(mix_kernel, out_shape=jax.ShapeDtypeStruct((blocks, capaci...  35.8 us
    all_gather x1, blocking collectives, scanned(): ends = lax.all_gather(ends, 'ctx')  8.89 us
    unnamed x21, local copies, waits for them, and re-layouts  8.34 us
    pallas_call x1, Pallas kernels, scanned(): pl.pallas_call(read_kernel, out_shape=jax.ShapeDtypeStruct((length,) + ti...  5.87 us
    pallas_call x1, Pallas kernels, scanned(): pl.pallas_call(end_kernel, out_shape=jax.ShapeDtypeStruct((count + 1,) +...  4.02 us
    unnamed x4, other arithmetic  2.94 us

profile of v2, /device:TPU:0, one launch (start us, length us, event | category | flops | bytes accessed | tf_op | source)
XLA Modules:
  0.0 121.9 jit_solution(2563964646394176926)
XLA Ops:
  0.0 0.0 copy-start.6
  0.0 0.0 copy-start.3
  0.0 0.0 copy-start.2
  0.0 1.0 convert_bitcast_fusion.1
  1.0 0.1 copy.53
  1.1 0.0 copy-start.5
  1.2 1.3 %copy.52 = f32[16,8,8,128]{3,2,1,0:T(8,128)S(1)} copy(f32[16,8,8,128]{3,1,2,0:T(8,128)} %bitcast.61) | data formatting | bytes 1048576
  2.5 0.0 copy-start.4
  2.5 0.9 bitcast_multiply_fusion.drive_ref
  3.4 0.9 negate_bitcast_fusion
  4.3 0.6 copy.55
  4.9 0.0 copy-done.4
  4.9 4.0 %end_states.1 = f32[17,8,128]{2,1,0:T(8,128)} custom-call(f32[128,8,128]{2,1,0:T(8,128)} %bitcast.49, f32[128,8,128]{2,1,0:T(8,128)} %bitcast_multiply_fusion.drive_ref, f32[16,8,128]{2,1,0:T(8,128)} %bitcast.59, f32[16,128]{1,0:T(8,128)} %in_ref.3), custom_call_target="tpu_custom_call" | custom-call | tf_op jit(solution)/shard_map/end_states/pallas_call | solution.py:113
  8.9 8.9 %all-gather = f32[68,8,128]{2,1,0:T(8,128)} all-gather(f32[17,8,128]{2,1,0:T(8,128)} %end_states.1), channel_id=2, replica_groups=mesh['ctx'=4,'exp'=4,'tp'=2] {'ctx'}, dimensions={0}, use_global_device_ids=true | all-gather | bytes 348160 | tf_op jit(solution)/shard_map/all_gather | solution.py:120
  17.8 1.0 convert_bitcast_fusion
  18.8 0.9 copy.54
  19.7 0.0 copy-done.5
  19.7 5.9 %read_states.1 = f32[128,8,128]{2,1,0:T(8,128)} custom-call(f32[128,8,128]{2,1,0:T(8,128)} %bitcast.50, f32[128,8,128]{2,1,0:T(8,128)} %bitcast_multiply_fusion.drive_ref, f32[128,8,128]{2,1,0:T(8,128)} %bitcast.54, f32[128,8,128]{2,1,0:T(8,128)} %bitcast.55, f32[8,128]{1,0:T(8,128)} %bitcast.64, f32[16,8,128]{2,1,0:T(8,128)} %bitcast.60, ...), custom_call_target="tpu_custom_call" | custom-call | tf_op jit(solution)/shard_map/read_states/pallas_call | solution.py:121
  25.6 1.1 convert_element_type.24
  26.7 0.0 copy-done.6
  26.7 0.1 copy.44
  26.8 0.1 eq.42
  27.0 1.2 %reduce-window.6 = s32[4,2,128]{2,1,0:T(2,128)S(1)} reduce-window(s32[4,2,128]{2,1,0:T(2,128)S(1)} %compare_convert_fusion, s32[]{:T(128)} %constant.6.clone.1), window={size=1x1x128 pad=0_0x0_0x127_0}, to_apply=%region_0.0 | reduce-window | flops 130048 | bytes 8196 | tf_op jit(solution)/shard_map/reduce-window
  28.2 0.1 slice.8
  28.3 0.1 copy.46
  28.4 0.1 copy.47
  28.5 0.1 add_bitcast_fusion
  28.6 0.1 eq.38
  28.8 0.1 reduce_sum.21
  28.9 0.1 copy.48
  29.0 0.1 convert_reduce_fusion
  29.1 0.1 copy.49
  29.2 0.1 copy.51.pick_ref
  29.4 0.0 copy-done.3
  29.4 0.0 copy-done.2
  29.4 0.0 copy-start.1
  29.4 2.2 %copy-done.1 = bf16[1024,2048]{1,0:T(8,128)(2,1)S(1)} copy-done((bf16[1024,2048]{1,0:T(8,128)(2,1)S(1)}, bf16[1024,2048]{1,0:T(8,128)(2,1)}, u32[]{:S(2)}) %copy-start.1) | copy-done | bytes 4194328
  31.6 35.8 %mix.1.rows_ref = bf16[4,128,2048]{2,1,0:T(8,128)(2,1)S(1)} custom-call(bf16[128,1024]{1,0:T(8,128)(2,1)S(1)} %bitcast.47, bf16[1024,2048]{1,0:T(8,128)(2,1)S(1)} %copy-done.1, bf16[128,256]{1,0:T(8,128)(2,1)S(1)} %copy-done.2, f32[1,2048]{1,0:T(1,128)S(1)} %bitcast.48, bf16[128,128]{1,0:T(8,128)(2,1)S(1)} %copy.51.pick_ref), custom_call_target="tpu_custom_call" | custom-call | tf_op jit(solution)/shard_map/mix/pallas_call | solution.py:446
  67.4 0.0 copy-start
  67.4 1.3 %copy-done = bf16[4,128,2048]{2,1,0:T(8,128)(2,1)} copy-done((bf16[4,128,2048]{2,1,0:T(8,128)(2,1)}, bf16[4,128,2048]{2,1,0:T(8,128)(2,1)S(1)}, u32[]{:S(2)}) %copy-start) | copy-done | bytes 2097176
  68.8 51.4 %experts.1 = bf16[128,1024]{1,0:T(8,128)(2,1)} custom-call(bf16[4,128,2048]{2,1,0:T(8,128)(2,1)} %copy-done, bf16[2048,1792]{1,0:T(8,128)(2,1)} %bitcast.51, bf16[2048,1792]{1,0:T(8,128)(2,1)} %bitcast.52, bf16[3584,1024]{1,0:T(8,128)(2,1)} %bitcast.53), custom_call_target="tpu_custom_call" | custom-call | tf_op jit(solution)/shard_map/experts/pallas_call | solution.py:293
  120.2 1.7 %copy.62 = bf16[1,1,128,1024]{3,2,1,0:T(8,128)(2,1)} copy(bf16[1,1,128,1024]{3,2,1,0:T(8,128)(2,1)} %bitcast.57) | data formatting | bytes 524288
  (8 shorter events, 0.1 us)
Async XLA Ops:
  0.0 26.7 %copy-start.6 = (s32[128,2]{0,1:T(2,128)S(1)}, s32[128,2]{0,1:T(2,128)}, u32[]{:S(2)}) copy-start(s32[128,2]{0,1:T(2,128)} %param.23) | copy-start | bytes 3076
  0.0 29.4 %copy-start.3 = (f32[2048]{0:T(1024)S(1)}, f32[2048]{0:T(1024)}, u32[]{:S(2)}) copy-start(f32[2048]{0:T(1024)} %param.24) | copy-start | bytes 24580
  0.0 29.4 %copy-start.2 = (bf16[128,256]{1,0:T(8,128)(2,1)S(1)}, bf16[128,256]{1,0:T(8,128)(2,1)}, u32[]{:S(2)}) copy-start(bf16[128,256]{1,0:T(8,128)(2,1)} %residual_ref.1) | copy-start | bytes 196612
  1.1 18.6 %copy-start.5 = (f32[16,8,8,128]{3,2,1,0:T(8,128)}, f32[16,8,8,128]{3,2,1,0:T(8,128)S(1)}, u32[]{:S(2)}) copy-start(f32[16,8,8,128]{3,2,1,0:T(8,128)S(1)} %copy.53) | copy-start | bytes 1572868
  2.5 2.4 %copy-start.4 = (f32[16,8,8,128]{3,2,1,0:T(8,128)}, f32[16,8,8,128]{3,2,1,0:T(8,128)S(1)}, u32[]{:S(2)}) copy-start(f32[16,8,8,128]{3,2,1,0:T(8,128)S(1)} %copy.52) | copy-start | bytes 1572868
  29.4 2.2 %copy-start.1 = (bf16[1024,2048]{1,0:T(8,128)(2,1)S(1)}, bf16[1024,2048]{1,0:T(8,128)(2,1)}, u32[]{:S(2)}) copy-start(bf16[1024,2048]{1,0:T(8,128)(2,1)} %weight_ref.1) | copy-start | bytes 12582916
  67.4 1.4 %copy-start = (bf16[4,128,2048]{2,1,0:T(8,128)(2,1)}, bf16[4,128,2048]{2,1,0:T(8,128)(2,1)S(1)}, u32[]{:S(2)}) copy-start(bf16[4,128,2048]{2,1,0:T(8,128)(2,1)S(1)} %mix.1.rows_ref) | copy-start | bytes 6291460

commit v3 on v2

--- a/solution.py
+++ b/solution.py
@@ -97,6 +97,49 @@
         return states
 
     lax.fori_loop(0, step_ref.shape[0], advance, incoming, unroll=4)
+
+
+def swap_kernel(end_ref, ends_ref, inbox, s_send, s_recv):
+    ctx, blocks = lax.axis_index("ctx"), lax.axis_size("ctx")
+    peers = [{"ctx": lax.rem(ctx + d, blocks)} for d in range(1, blocks)]
+    greet(peers)
+    copies = [
+        pltpu.make_async_remote_copy(
+            src_ref=end_ref,
+            dst_ref=inbox.at[d],
+            send_sem=s_send.at[d],
+            recv_sem=s_recv.at[d],
+            device_id=peer,
+            device_id_type=MESH,
+        )
+        for d, peer in enumerate(peers)
+    ]
+    for copy in copies:
+        copy.start()
+    ends_ref[ctx] = end_ref[...]
+    for d, copy in enumerate(copies):
+        copy.wait_recv()
+        ends_ref[lax.rem(ctx - d - 1 + blocks, blocks)] = inbox[d]
+    for copy in copies:
+        copy.wait_send()
+
+
+def swapped(ends):
+    blocks = lax.axis_size("ctx")
+    vmem, dma = pl.BlockSpec(memory_space=pltpu.VMEM), pltpu.SemaphoreType.DMA
+    return pl.pallas_call(
+        swap_kernel,
+        out_shape=jax.ShapeDtypeStruct((blocks,) + ends.shape, ends.dtype),
+        in_specs=[vmem],
+        out_specs=vmem,
+        scratch_shapes=[
+            pltpu.VMEM((blocks - 1,) + ends.shape, ends.dtype),
+            dma((blocks - 1,)),
+            dma((blocks - 1,)),
+        ],
+        compiler_params=pltpu.CompilerParams(collective_id=2, has_side_effects=True),
+        name="swap",
+    )(ends)
 
 
 def scanned(mamba_in, gate_in, step_size, input_proj, output_proj, decay_log, skip_gain):
@@ -117,7 +160,7 @@
         out_specs=vmem,
         name="end_states",
     )(step, drive, rate, input_proj)
-    ends = lax.all_gather(ends, "ctx")
+    ends = swapped(ends)
     gated = pl.pallas_call(
         read_kernel,
         out_shape=jax.ShapeDtypeStruct((length,) + tile, jnp.float32),

time: 123 us -> 125 us (1.016)
  Pallas kernels: 97.1 us -> 108 us
  blocking collectives: 8.89 us -> 0 us
    all_gather x1 -> x0, blocking collectives: 8.89 us -> none  [scanned(): ends = lax.all_gather(ends, 'ctx')]
    pallas_call x0 -> x1, Pallas kernels: none -> 8.12 us  [swapped(): pl.pallas_call(swap_kernel, out_shape=jax.ShapeDtypeStruct((blocks,) + en...]
    pallas_call x1, Pallas kernels: 51.4 us -> 53.1 us  [experts_tiled(): pl.pallas_call(expert_kernel, out_shape=jax.ShapeDtypeStruct((capacity, w...]
where the time goes in v3:
time: 125 us; the launch traced here: 124 us
  Pallas kernels  108 us (86%)
  local copies, waits for them, and re-layouts  9.32 us (7%)
  other arithmetic  6.34 us (5%)
    pallas_call x1, Pallas kernels, experts_tiled(): pl.pallas_call(expert_kernel, out_shape=jax.ShapeDtypeStruct((capacity, w...  53.1 us
    pallas_call x1, Pallas kernels, mixed_slots(): pl.pallas_call(mix_kernel, out_shape=jax.ShapeDtypeStruct((blocks, capaci...  36.9 us
    unnamed x21, local copies, waits for them, and re-layouts  8.34 us
    pallas_call x1, Pallas kernels, swapped(): pl.pallas_call(swap_kernel, out_shape=jax.ShapeDtypeStruct((blocks,) + en...  8.12 us
    pallas_call x1, Pallas kernels, scanned(): pl.pallas_call(read_kernel, out_shape=jax.ShapeDtypeStruct((length,) + ti...  5.87 us
    pallas_call x1, Pallas kernels, scanned(): pl.pallas_call(end_kernel, out_shape=jax.ShapeDtypeStruct((count + 1,) +...  4.02 us
    unnamed x4, other arithmetic  2.95 us

profile of v3, /device:TPU:0, one launch (start us, length us, event | category | flops | bytes accessed | tf_op | source)
XLA Modules:
  0.0 123.8 jit_solution(14279444991388037852)
XLA Ops:
  0.0 0.0 copy-start.6
  0.0 0.0 copy-start.3
  0.0 0.0 copy-start.2
  0.0 1.0 convert_bitcast_fusion.1
  1.0 0.1 copy.45
  1.1 0.0 copy-start.5
  1.2 1.3 %copy.44 = f32[16,8,8,128]{3,2,1,0:T(8,128)S(1)} copy(f32[16,8,8,128]{3,1,2,0:T(8,128)} %bitcast.59) | data formatting | bytes 1048576
  2.5 0.0 copy-start.4
  2.5 0.9 bitcast_multiply_fusion.drive_ref
  3.4 0.9 negate_bitcast_fusion
  4.3 0.6 copy.47
  4.9 0.0 copy-done.4
  4.9 4.0 %end_states.1.end_ref = f32[17,8,128]{2,1,0:T(8,128)} custom-call(f32[128,8,128]{2,1,0:T(8,128)} %bitcast.48, f32[128,8,128]{2,1,0:T(8,128)} %bitcast_multiply_fusion.drive_ref, f32[16,8,128]{2,1,0:T(8,128)} %bitcast.57, f32[16,128]{1,0:T(8,128)} %in_ref.3), custom_call_target="tpu_custom_call" | custom-call | tf_op jit(solution)/shard_map/end_states/pallas_call | solution.py:156
  8.9 8.1 %swap.1.ends_ref = f32[4,17,8,128]{3,2,1,0:T(8,128)} custom-call(f32[17,8,128]{2,1,0:T(8,128)} %end_states.1.end_ref), custom_call_target="tpu_custom_call" | custom-call | tf_op jit(solution)/shard_map/swap/pallas_call | solution.py:130
  17.1 1.0 convert_bitcast_fusion
  18.1 0.9 copy.46
  19.0 0.0 copy-done.5
  19.0 5.9 %read_states.1 = f32[128,8,128]{2,1,0:T(8,128)} custom-call(f32[128,8,128]{2,1,0:T(8,128)} %bitcast.49, f32[128,8,128]{2,1,0:T(8,128)} %bitcast_multiply_fusion.drive_ref, f32[128,8,128]{2,1,0:T(8,128)} %bitcast.53, f32[128,8,128]{2,1,0:T(8,128)} %bitcast.54, f32[8,128]{1,0:T(8,128)} %bitcast.62, f32[16,8,128]{2,1,0:T(8,128)} %bitcast.58, ...), custom_call_target="tpu_custom_call" | custom-call | tf_op jit(solution)/shard_map/read_states/pallas_call | solution.py:164
  24.8 1.1 convert_element_type.24
  26.0 0.0 copy-done.6
  26.0 0.1 copy.36
  26.1 0.1 eq.42
  26.2 1.2 reduce-window.6
  27.5 0.1 slice.8
  27.5 0.1 copy.38
  27.7 0.1 copy.39
  27.8 0.1 add_bitcast_fusion
  27.9 0.1 eq.38
  28.0 0.1 reduce_sum.21
  28.2 0.1 copy.40
  28.2 0.1 convert_reduce_fusion
  28.4 0.1 copy.41
  28.5 0.1 copy.43.pick_ref
  28.6 0.0 copy-done.3
  28.6 0.0 copy-done.2
  28.6 0.0 copy-start.1
  28.6 2.2 %copy-done.1 = bf16[1024,2048]{1,0:T(8,128)(2,1)S(1)} copy-done((bf16[1024,2048]{1,0:T(8,128)(2,1)S(1)}, bf16[1024,2048]{1,0:T(8,128)(2,1)}, u32[]{:S(2)}) %copy-start.1) | copy-done | bytes 4194328
  30.8 36.9 %mix.1.rows_ref = bf16[4,128,2048]{2,1,0:T(8,128)(2,1)S(1)} custom-call(bf16[128,1024]{1,0:T(8,128)(2,1)S(1)} %bitcast.46, bf16[1024,2048]{1,0:T(8,128)(2,1)S(1)} %copy-done.1, bf16[128,256]{1,0:T(8,128)(2,1)S(1)} %copy-done.2, f32[1,2048]{1,0:T(1,128)S(1)} %bitcast.47, bf16[128,128]{1,0:T(8,128)(2,1)S(1)} %copy.43.pick_ref), custom_call_target="tpu_custom_call" | custom-call | tf_op jit(solution)/shard_map/mix/pallas_call | solution.py:489
  67.7 0.0 copy-start
  67.7 1.3 %copy-done = bf16[4,128,2048]{2,1,0:T(8,128)(2,1)} copy-done((bf16[4,128,2048]{2,1,0:T(8,128)(2,1)}, bf16[4,128,2048]{2,1,0:T(8,128)(2,1)S(1)}, u32[]{:S(2)}) %copy-start) | copy-done | bytes 2097176
  69.0 53.1 %experts.1 = bf16[128,1024]{1,0:T(8,128)(2,1)} custom-call(bf16[4,128,2048]{2,1,0:T(8,128)(2,1)} %copy-done, bf16[2048,1792]{1,0:T(8,128)(2,1)} %bitcast.50, bf16[2048,1792]{1,0:T(8,128)(2,1)} %bitcast.51, bf16[3584,1024]{1,0:T(8,128)(2,1)} %bitcast.52), custom_call_target="tpu_custom_call" | custom-call | tf_op jit(solution)/shard_map/experts/pallas_call | solution.py:336
  122.1 1.7 %copy.54 = bf16[1,1,128,1024]{3,2,1,0:T(8,128)(2,1)} copy(bf16[1,1,128,1024]{3,2,1,0:T(8,128)(2,1)} %bitcast.55) | data formatting | bytes 524288
  (8 shorter events, 0.1 us)
Async XLA Ops:
  0.0 26.0 %copy-start.6 = (s32[128,2]{0,1:T(2,128)S(1)}, s32[128,2]{0,1:T(2,128)}, u32[]{:S(2)}) copy-start(s32[128,2]{0,1:T(2,128)} %param.23) | copy-start | bytes 3076
  0.0 28.6 %copy-start.3 = (f32[2048]{0:T(1024)S(1)}, f32[2048]{0:T(1024)}, u32[]{:S(2)}) copy-start(f32[2048]{0:T(1024)} %param.24) | copy-start | bytes 24580
  0.0 28.6 %copy-start.2 = (bf16[128,256]{1,0:T(8,128)(2,1)S(1)}, bf16[128,256]{1,0:T(8,128)(2,1)}, u32[]{:S(2)}) copy-start(bf16[128,256]{1,0:T(8,128)(2,1)} %residual_ref.1) | copy-start | bytes 196612
  1.1 17.8 %copy-start.5 = (f32[16,8,8,128]{3,2,1,0:T(8,128)}, f32[16,8,8,128]{3,2,1,0:T(8,128)S(1)}, u32[]{:S(2)}) copy-start(f32[16,8,8,128]{3,2,1,0:T(8,128)S(1)} %copy.45) | copy-start | bytes 1572868
  2.5 2.4 %copy-start.4 = (f32[16,8,8,128]{3,2,1,0:T(8,128)}, f32[16,8,8,128]{3,2,1,0:T(8,128)S(1)}, u32[]{:S(2)}) copy-start(f32[16,8,8,128]{3,2,1,0:T(8,128)S(1)} %copy.44) | copy-start | bytes 1572868
  28.6 2.2 %copy-start.1 = (bf16[1024,2048]{1,0:T(8,128)(2,1)S(1)}, bf16[1024,2048]{1,0:T(8,128)(2,1)}, u32[]{:S(2)}) copy-start(bf16[1024,2048]{1,0:T(8,128)(2,1)} %weight_ref.1) | copy-start | bytes 12582916
  67.7 1.4 %copy-start = (bf16[4,128,2048]{2,1,0:T(8,128)(2,1)}, bf16[4,128,2048]{2,1,0:T(8,128)(2,1)S(1)}, u32[]{:S(2)}) copy-start(bf16[4,128,2048]{2,1,0:T(8,128)(2,1)S(1)} %mix.1.rows_ref) | copy-start | bytes 6291460
